TPU v7x, 512 devices: a whole 4x8x8 slice. The times are simulated.
512 devices in a mesh: rec: 128 (over y, z, core), grp: 4 (over x).
Axes of the slice: x: 4, y: 8, z: 8, core: 2. Of those that a mesh axis runs over, the one named last changes fastest.
Arguments:
- conv_in: bfloat16 [4, 131072, 512], P('grp', 'rec'), may hold values from -6 to 6
- conv5_weight: bfloat16 [1536, 512], P(None, 'grp'), may hold values from -0.15625 to 0.15625
- conv6_weight: bfloat16 [1024, 512], P(None, 'grp'), may hold values from -0.1875 to 0.1875
- conv7_weight: bfloat16 [1024, 512], P(None, 'grp'), may hold values from -0.1875 to 0.1875
- norm_gain: float32 [512], replicated, may hold values from 0.1 to 1.9
- norm_bias: float32 [512], replicated, may hold values from -3 to 3
- proj_weight: bfloat16 [512, 768], P(None, 'grp'), may hold values from -0.25 to 0.25
- proj_bias: float32 [768], replicated, may hold values from -3 to 3
- rec_length: int32 [4], P('grp'), may hold values from 8192 to 16384, as said below
- assign: int32 [3, 4, 16384], P(None, 'grp', 'rec'), may hold values from 0 to 999, as said below
- centroid_init: float32 [1024, 768], P('rec'), may hold values from -6 to 6
- prior_count: float32 [1024], P('rec'), may hold values from 50 to 500
Outputs:
- distortion: float32 [3, 4, 16384], P(None, 'grp', 'rec')
- centroids: float32 [1024, 768], P('rec')
Inputs may be any that keep to these rules, and one draw needn't show every extreme that they name: `rec_length`: some recording has all 16384 frames. `assign`: clusters form blocks of 8 consecutive ids (block b holds ids b * 8 to b * 8 + 7). In each iteration the 128 frames of one device name clusters of one block at most 2 times, and in each iteration some block is named exactly 2 times by the frames of every device of one recording.
All inputs are finite; a program needn't handle non-finite values.
Results may differ from a plain program's by a relative error of at most 0.0013.
Values may be sent and summed in bfloat16 or wider, within the bound.
A program may use at most 64 MiB of HBM per device.

v0:
```python
import jax
import jax.numpy as jnp
from jax import lax
from jax.sharding import PartitionSpec as P

K = 1000
ITERS = 3


def shifted(value, axis, steps):
    count = lax.axis_size(axis)
    initial, last = (max(0, -steps), min(count, count - steps))
    return lax.ppermute(value, axis, [(source, source + steps) for source in range(initial, last)])


def linear(inputs, weight):
    return jnp.dot(
        inputs,
        lax.all_gather(weight, "grp", axis=1, tiled=True),
        preferred_element_type=jnp.float32,
    )


def conv_layer(inputs, weight):
    return jax.nn.gelu(linear(inputs, weight), approximate=False).astype(jnp.bfloat16)


def shards(
    conv_in,
    conv5_weight,
    conv6_weight,
    conv7_weight,
    norm_gain,
    norm_bias,
    proj_weight,
    proj_bias,
    rec_length,
    assign,
    centroid_init,
    prior_count,
):
    signal = conv_in[0]
    sample_rows = signal.shape[0]
    channels = signal.shape[1]
    next_row = shifted(signal[:1], "rec", -1)
    paired = signal.reshape(sample_rows // 2, 2 * channels)
    trailing = jnp.concatenate([signal[2::2], next_row], 0)
    stacked = jnp.concatenate([paired, trailing], 1)
    hidden = conv_layer(stacked, conv5_weight)
    hidden = conv_layer(hidden.reshape(-1, 2 * channels), conv6_weight)
    hidden = conv_layer(hidden.reshape(-1, 2 * channels), conv7_weight)
    hidden_wide = hidden.astype(jnp.float32)
    average = jnp.mean(hidden_wide, axis=-1, keepdims=True)
    variance = jnp.mean((hidden_wide - average) ** 2, axis=-1, keepdims=True)
    normed = ((hidden_wide - average) * lax.rsqrt(variance + 1e-05) * norm_gain + norm_bias).astype(
        jnp.bfloat16
    )
    frames = (linear(normed, proj_weight) + proj_bias).astype(jnp.bfloat16)
    frame_count = frames.shape[0]
    feature_width = frames.shape[1]
    ranks_total = lax.axis_size("rec")
    slice_rows = centroid_init.shape[0]
    owners_used = (K + slice_rows - 1) // slice_rows
    capacity = max(2, (5 * frame_count + 4 * owners_used - 1) // (4 * owners_used))
    position = lax.axis_index("rec") * frame_count + jnp.arange(frame_count, dtype=jnp.int32)
    is_live = (position < rec_length[0]).astype(jnp.int32)
    frame_index = jnp.arange(frame_count, dtype=jnp.int32)
    earlier = (frame_index[None, :] < frame_index[:, None]).astype(jnp.bfloat16)
    owner_ids = jnp.arange(ranks_total, dtype=jnp.int32)
    cluster_ids = jnp.arange(slice_rows, dtype=jnp.int32)
    frames_wide = frames.astype(jnp.float32)
    centroid = centroid_init
    counts = prior_count
    results = []
    for iteration in range(ITERS):
        chosen = assign[iteration, 0]
        owner_id = chosen // slice_rows
        inner_id = chosen - owner_id * slice_rows
        owner_hot = (owner_id[:, None] == owner_ids[None, :]).astype(jnp.bfloat16)
        before = jnp.dot(earlier, owner_hot, preferred_element_type=jnp.float32)
        slot_id = jnp.sum(before * owner_hot.astype(jnp.float32), axis=1).astype(jnp.int32)
        target = owner_id * capacity + slot_id
        slot_total = ranks_total * capacity
        send_rows = jnp.zeros((slot_total, feature_width), jnp.bfloat16).at[target].set(frames)
        send_ids = jnp.full((slot_total,), -1, jnp.int32).at[target].set(inner_id)
        send_live = jnp.zeros((slot_total,), jnp.int32).at[target].set(is_live)
        got_rows, got_ids, got_live = (
            lax.all_to_all(
                send_rows.reshape(ranks_total, capacity, feature_width),
                "rec",
                split_axis=0,
                concat_axis=0,
                tiled=True,
            ),
            lax.all_to_all(
                send_ids.reshape(ranks_total, capacity),
                "rec",
                split_axis=0,
                concat_axis=0,
                tiled=True,
            ),
            lax.all_to_all(
                send_live.reshape(ranks_total, capacity),
                "rec",
                split_axis=0,
                concat_axis=0,
                tiled=True,
            ),
        )
        got_rows = got_rows.reshape(slot_total, feature_width)
        got_ids = got_ids.reshape(slot_total)
        got_live = got_live.reshape(slot_total)
        member = ((got_ids[:, None] == cluster_ids[None, :]) & (got_live[:, None] > 0)).astype(
            jnp.bfloat16
        )
        partial_value = jnp.dot(member.T, got_rows, preferred_element_type=jnp.float32)
        hit_count = jnp.sum(member.astype(jnp.float32), axis=0)
        coded = centroid.astype(jnp.bfloat16)
        codebook = lax.all_gather(coded, "rec", axis=0, tiled=True)
        picked = jnp.take(codebook, chosen, axis=0).astype(jnp.float32)
        gap_value = frames_wide - picked
        results.append(jnp.sum(gap_value * gap_value, axis=1) / feature_width)
        summed, hit_total = lax.psum((partial_value, hit_count), "grp")
        updated = counts + hit_total
        centroid = (counts[:, None] * centroid + summed) / updated[:, None]
        counts = updated
    distortion = jnp.stack(results, 0)[:, None, :]
    return (distortion, centroid)


def solution(mesh):
    in_specs = (
        P("grp", "rec", None),
        P(None, "grp"),
        P(None, "grp"),
        P(None, "grp"),
        P(),
        P(),
        P(None, "grp"),
        P(),
        P("grp"),
        P(None, "grp", "rec"),
        P("rec", None),
        P("rec"),
    )
    out_specs = (P(None, "grp", "rec"), P("rec", None))
    return jax.shard_map(shards, mesh=mesh, in_specs=in_specs, out_specs=out_specs, check_vma=False)
```

profile of v0, /device:TPU:1, one launch (start us, length us, event | category | flops | bytes accessed | tf_op | source)
XLA Modules:
  0.0 582.5 jit_solution(9825672385246203431)
XLA Ops:
  12.4 18.4 %all-to-all-start.3 = ((s32[128,1,2]{2,1,0:T(1,128)}), s32[128,1,2]{2,1,0:T(1,128)S(1)}, u32[]{:S(2)}, u32[]{:S(2)}) async-start(s32[128,1,2]{2,1,0:T(1,128)} %bitcast.16), calls=%async_computation.3 | async-start | bytes 131072 | tf_op jit(solution)/shard_map/all_to_all | solution.py:95
  34.4 15.8 %all_gather.24 = bf16[512,768]{0,1:T(8,128)(2,1)S(1)} all-gather(bf16[512,192]{0,1:T(8,128)(2,1)} %param.20), channel_id=1, replica_groups=mesh['rec'=128,'grp'=4] {'grp'}, dimensions={1}, use_global_device_ids=true | all-gather | bytes 983040 | tf_op jit(solution)/shard_map/all_gather | solution.py:19
  61.2 4.9 fusion.12
  66.3 20.3 %all-gather.9.cloned.1.call-done = bf16[1024,512]{1,0:T(8,128)(2,1)} async-done(((bf16[1024,128]{1,0:T(8,128)(2,1)}), bf16[1024,512]{1,0:T(8,128)(2,1)}) %all-gather.9.cloned.1.call-update) | async-done | bytes 1048592 | tf_op jit(solution)/shard_map/all_gather | solution.py:19
  89.4 15.9 %all-to-all-start.6 = ((s32[128,1,2]{2,1,0:T(1,128)}), s32[128,1,2]{2,1,0:T(1,128)S(1)}, u32[]{:S(2)}, u32[]{:S(2)}) async-start(s32[128,1,2]{2,1,0:T(1,128)} %bitcast.23), calls=%async_computation.6 | async-start | bytes 131072 | tf_op jit(solution)/shard_map/all_to_all | solution.py:95
  105.3 15.1 %all-gather.11.cloned.1.call-done = bf16[1024,512]{1,0:T(8,128)(2,1)} async-done(((bf16[1024,128]{1,0:T(8,128)(2,1)}), bf16[1024,512]{1,0:T(8,128)(2,1)}) %all-gather.11.cloned.1.call-update) | async-done | bytes 1048592 | tf_op jit(solution)/shard_map/all_gather | solution.py:19
  122.6 15.9 %all-to-all-start.4 = ((s32[128,1,2]{2,1,0:T(1,128)}), s32[128,1,2]{2,1,0:T(1,128)S(1)}, u32[]{:S(2)}, u32[]{:S(2)}) async-start(s32[128,1,2]{2,1,0:T(1,128)} %bitcast.17), calls=%async_computation.4 | async-start | bytes 131072 | tf_op jit(solution)/shard_map/all_to_all | solution.py:102
  138.5 11.5 %all-to-all-done.4 = s32[128,1,2]{2,1,0:T(1,128)S(1)} async-done(((s32[128,1,2]{2,1,0:T(1,128)}), s32[128,1,2]{2,1,0:T(1,128)S(1)}, u32[]{:S(2)}, u32[]{:S(2)}) %all-to-all-start.4) | async-done | bytes 1056 | tf_op jit(solution)/shard_map/all_to_all | solution.py:102
  150.1 5.6 all-to-all-start.7
  155.9 11.5 %all-to-all-done.7 = s32[128,1,2]{2,1,0:T(1,128)S(1)} async-done(((s32[128,1,2]{2,1,0:T(1,128)}), s32[128,1,2]{2,1,0:T(1,128)S(1)}, u32[]{:S(2)}, u32[]{:S(2)}) %all-to-all-start.7) | async-done | bytes 1056 | tf_op jit(solution)/shard_map/all_to_all | solution.py:102
  167.4 5.7 all-to-all-start
  173.1 11.7 %all-to-all-done = s32[128,1,2]{2,1,0:T(1,128)S(1)} async-done(((s32[128,1,2]{2,1,0:T(1,128)}), s32[128,1,2]{2,1,0:T(1,128)S(1)}, u32[]{:S(2)}, u32[]{:S(2)}) %all-to-all-start) | async-done | bytes 1056 | tf_op jit(solution)/shard_map/all_to_all | solution.py:95
  184.8 5.7 all-to-all-start.1
  193.0 9.1 %all-to-all-done.1 = s32[128,1,2]{2,1,0:T(1,128)S(1)} async-done(((s32[128,1,2]{2,1,0:T(1,128)}), s32[128,1,2]{2,1,0:T(1,128)S(1)}, u32[]{:S(2)}, u32[]{:S(2)}) %all-to-all-start.1) | async-done | bytes 1056 | tf_op jit(solution)/shard_map/all_to_all | solution.py:102
  202.1 5.7 all-to-all-start.5
  210.0 14.8 %all-to-all-done.5 = bf16[128,2,768]{2,1,0:T(2,128)(2,1)S(1)} async-done(((bf16[128,2,768]{2,1,0:T(2,128)(2,1)}), bf16[128,2,768]{2,1,0:T(2,128)(2,1)S(1)}, u32[]{:S(2)}, u32[]{:S(2)}) %all-to-all-start.5) | async-done | bytes 393248 | tf_op jit(solution)/shard_map/all_to_all | solution.py:88
  224.8 7.1 %all-to-all-start.8 = ((bf16[128,2,768]{2,1,0:T(2,128)(2,1)}), bf16[128,2,768]{2,1,0:T(2,128)(2,1)S(1)}, u32[]{:S(2)}, u32[]{:S(2)}) async-start(bf16[128,2,768]{2,1,0:T(2,128)(2,1)} %reshape.452), calls=%async_computation.8 | async-start | bytes 786432 | tf_op jit(solution)/shard_map/all_to_all | solution.py:88
  238.1 10.7 %all-to-all-done.8 = bf16[128,2,768]{2,1,0:T(2,128)(2,1)S(1)} async-done(((bf16[128,2,768]{2,1,0:T(2,128)(2,1)}), bf16[128,2,768]{2,1,0:T(2,128)(2,1)S(1)}, u32[]{:S(2)}, u32[]{:S(2)}) %all-to-all-start.8) | async-done | bytes 393248 | tf_op jit(solution)/shard_map/all_to_all | solution.py:88
  248.8 7.1 %all-to-all-start.2 = ((bf16[128,2,768]{2,1,0:T(2,128)(2,1)}), bf16[128,2,768]{2,1,0:T(2,128)(2,1)S(1)}, u32[]{:S(2)}, u32[]{:S(2)}) async-start(bf16[128,2,768]{2,1,0:T(2,128)(2,1)} %reshape.448), calls=%async_computation.2 | async-start | bytes 786432 | tf_op jit(solution)/shard_map/all_to_all | solution.py:88
  259.6 13.2 %all-to-all-done.2 = bf16[128,2,768]{2,1,0:T(2,128)(2,1)S(1)} async-done(((bf16[128,2,768]{2,1,0:T(2,128)(2,1)}), bf16[128,2,768]{2,1,0:T(2,128)(2,1)S(1)}, u32[]{:S(2)}, u32[]{:S(2)}) %all-to-all-start.2) | async-done | bytes 393248 | tf_op jit(solution)/shard_map/all_to_all | solution.py:88
  273.8 42.7 %all-reduce.3.cloned.1.call-done = (f32[8]{0:T(128)}, f32[8,768]{1,0:T(8,128)}, f32[8,768]{1,0:T(8,128)}, f32[8]{0:T(128)}, f32[8,768]{1,0:T(8,128)}, /*index=5*/f32[8]{0:T(128)}) async-done(((f32[8]{0:T(128)}, f32[8,768]{1,0:T(8,128)}, f32[8,768]{1,0:T(8,128)}, f32[8]{0:T(128)}, f32[8,768]{1,0:T(8,128)}, /*index=5*/f32[8]{0:T(128)}), (f32[8]{0:T(128)}, f32[8,768]{1,0:T(8,128)}, f32[8,768]{1,0:T(8,128)}, ...) | async-done | bytes 73840 | tf_op jit(solution)/shard_map/psum | solution.py:123
  320.0 85.9 %all-gather.15.cloned.1.call-done = bf16[1024,768]{1,0:T(8,128)(2,1)} async-done(((bf16[8,768]{1,0:T(8,128)(2,1)}), bf16[1024,768]{1,0:T(8,128)(2,1)}) %all-gather.15.cloned.1.call-update) | async-done | bytes 1572880 | tf_op jit(solution)/shard_map/all_gather | solution.py:119
  408.5 80.4 %all-gather.17.cloned.1.call-done = bf16[1024,768]{1,0:T(8,128)(2,1)} async-done(((bf16[8,768]{1,0:T(8,128)(2,1)}), bf16[1024,768]{1,0:T(8,128)(2,1)}) %all-gather.17.cloned.1.call-update) | async-done | bytes 1572880 | tf_op jit(solution)/shard_map/all_gather | solution.py:119
  491.5 80.6 %all-gather.13.cloned.1.call-done = bf16[1024,768]{1,0:T(8,128)(2,1)} async-done(((bf16[8,768]{1,0:T(8,128)(2,1)}), bf16[1024,768]{1,0:T(8,128)(2,1)}) %all-gather.13.cloned.1.call-update) | async-done | bytes 1572880 | tf_op jit(solution)/shard_map/all_gather | solution.py:119
  (103 shorter events, 52.0 us)
Async XLA Ops:
  7.2 43.7 %copy-start = (bf16[1,1024,512]{2,1,0:T(8,128)(2,1)S(1)}, bf16[1,1024,512]{2,1,0:T(8,128)(2,1)}, u32[]{:S(2)}) copy-start(bf16[1,1024,512]{2,1,0:T(8,128)(2,1)} %param.14) | copy-start | bytes 3145732
  7.2 54.0 %all-gather.7.cloned.1.call-start = ((), (), s32[]{:S(2)}) async-start(), calls=%async_computation.9 | async-start | bytes 1966080 | tf_op jit(solution)/shard_map/all_gather | solution.py:19
  7.9 78.7 %all-gather.9.cloned.1.call-start = ((), (), s32[]{:S(2)}) async-start(), calls=%async_computation.10 | async-start | bytes 1310720 | tf_op jit(solution)/shard_map/all_gather | solution.py:19
  12.4 77.0 %all-to-all-start.3 = ((s32[128,1,2]{2,1,0:T(1,128)}), s32[128,1,2]{2,1,0:T(1,128)S(1)}, u32[]{:S(2)}, u32[]{:S(2)}) async-start(s32[128,1,2]{2,1,0:T(1,128)} %bitcast.16), calls=%async_computation.3 | async-start | bytes 131072 | tf_op jit(solution)/shard_map/all_to_all | solution.py:95
  30.8 89.6 %all-gather.11.cloned.1.call-start = ((), (), s32[]{:S(2)}) async-start(), calls=%async_computation.11 | async-start | bytes 1310720 | tf_op jit(solution)/shard_map/all_gather | solution.py:19
  31.6 29.6 %collective-permute-start = (bf16[1,512]{1,0:T(2,128)(2,1)S(1)}, bf16[1,512]{1,0:T(2,128)(2,1)S(1)}, u32[]{:S(2)}, u32[]{:S(2)}) collective-permute-start(bf16[1,512]{1,0:T(2,128)(2,1)S(1)} %slice_bitcast_fusion), channel_id=1, source_target_pairs={{4,0},{8,4},{12,8},{16,12},{20,16},{24,20},{28,24},{32,28},{36,32}... | collective-permute-start | bytes 3080 | tf_op jit(solution)/shard_map/ppermute | solution.py:13
  89.4 33.2 %all-to-all-start.6 = ((s32[128,1,2]{2,1,0:T(1,128)}), s32[128,1,2]{2,1,0:T(1,128)S(1)}, u32[]{:S(2)}, u32[]{:S(2)}) async-start(s32[128,1,2]{2,1,0:T(1,128)} %bitcast.23), calls=%async_computation.6 | async-start | bytes 131072 | tf_op jit(solution)/shard_map/all_to_all | solution.py:95
  105.3 85.1 %copy-start.4 = (f32[768]{0:T(1024)S(1)}, f32[768]{0:T(1024)}, u32[]{:S(2)}) copy-start(f32[768]{0:T(1024)} %param.21) | copy-start | bytes 9220
  105.3 85.1 %copy-start.5 = (f32[512]{0:T(512)S(1)}, f32[512]{0:T(512)}, u32[]{:S(2)}) copy-start(f32[512]{0:T(512)} %param.19) | copy-start | bytes 6148
  105.3 85.1 %copy-start.6 = (f32[512]{0:T(512)S(1)}, f32[512]{0:T(512)}, u32[]{:S(2)}) copy-start(f32[512]{0:T(512)} %param.18) | copy-start | bytes 6148
  122.6 27.4 %all-to-all-start.4 = ((s32[128,1,2]{2,1,0:T(1,128)}), s32[128,1,2]{2,1,0:T(1,128)S(1)}, u32[]{:S(2)}, u32[]{:S(2)}) async-start(s32[128,1,2]{2,1,0:T(1,128)} %bitcast.17), calls=%async_computation.4 | async-start | bytes 131072 | tf_op jit(solution)/shard_map/all_to_all | solution.py:102
  150.1 17.3 %all-to-all-start.7 = ((s32[128,1,2]{2,1,0:T(1,128)}), s32[128,1,2]{2,1,0:T(1,128)S(1)}, u32[]{:S(2)}, u32[]{:S(2)}) async-start(s32[128,1,2]{2,1,0:T(1,128)} %bitcast.24), calls=%async_computation.7 | async-start | bytes 131072 | tf_op jit(solution)/shard_map/all_to_all | solution.py:102
  167.4 17.4 %all-to-all-start = ((s32[128,1,2]{2,1,0:T(1,128)}), s32[128,1,2]{2,1,0:T(1,128)S(1)}, u32[]{:S(2)}, u32[]{:S(2)}) async-start(s32[128,1,2]{2,1,0:T(1,128)} %bitcast.8), calls=%async_computation | async-start | bytes 131072 | tf_op jit(solution)/shard_map/all_to_all | solution.py:95
  184.8 17.3 %all-to-all-start.1 = ((s32[128,1,2]{2,1,0:T(1,128)}), s32[128,1,2]{2,1,0:T(1,128)S(1)}, u32[]{:S(2)}, u32[]{:S(2)}) async-start(s32[128,1,2]{2,1,0:T(1,128)} %bitcast.10), calls=%async_computation.1 | async-start | bytes 131072 | tf_op jit(solution)/shard_map/all_to_all | solution.py:102
  202.1 22.6 %all-to-all-start.5 = ((bf16[128,2,768]{2,1,0:T(2,128)(2,1)}), bf16[128,2,768]{2,1,0:T(2,128)(2,1)S(1)}, u32[]{:S(2)}, u32[]{:S(2)}) async-start(bf16[128,2,768]{2,1,0:T(2,128)(2,1)} %reshape.450), calls=%async_computation.5 | async-start | bytes 786432 | tf_op jit(solution)/shard_map/all_to_all | solution.py:88
  224.8 24.0 %all-to-all-start.8 = ((bf16[128,2,768]{2,1,0:T(2,128)(2,1)}), bf16[128,2,768]{2,1,0:T(2,128)(2,1)S(1)}, u32[]{:S(2)}, u32[]{:S(2)}) async-start(bf16[128,2,768]{2,1,0:T(2,128)(2,1)} %reshape.452), calls=%async_computation.8 | async-start | bytes 786432 | tf_op jit(solution)/shard_map/all_to_all | solution.py:88
  248.8 24.0 %all-to-all-start.2 = ((bf16[128,2,768]{2,1,0:T(2,128)(2,1)}), bf16[128,2,768]{2,1,0:T(2,128)(2,1)S(1)}, u32[]{:S(2)}, u32[]{:S(2)}) async-start(bf16[128,2,768]{2,1,0:T(2,128)(2,1)} %reshape.448), calls=%async_computation.2 | async-start | bytes 786432 | tf_op jit(solution)/shard_map/all_to_all | solution.py:88
  255.9 60.6 %all-reduce.3.cloned.1.call-start = ((), (), s32[]{:S(2)}) async-start(), calls=%async_computation.15 | async-start | bytes 150528 | tf_op jit(solution)/shard_map/psum | solution.py:123
  257.8 58.7 %copy-start.3 = (f32[8]{0:T(128)S(1)}, f32[8]{0:T(128)}, u32[]{:S(2)}) copy-start(f32[8]{0:T(128)} %param.25) | copy-start | bytes 100
  257.8 59.3 %copy-start.1 = (f32[8,768]{1,0:T(8,128)S(1)}, f32[8,768]{1,0:T(8,128)}, u32[]{:S(2)}) copy-start(f32[8,768]{1,0:T(8,128)} %param.24) | copy-start | bytes 73732
  257.8 62.1 %copy-start.2 = (s32[3,1,128]{2,1,0:T(1,128)S(1)}, s32[3,1,128]{2,1,0:T(1,128)}, u32[]{:S(2)}) copy-start(s32[3,1,128]{2,1,0:T(1,128)} %param.23) | copy-start | bytes 4612
  273.8 132.2 %all-gather.15.cloned.1.call-start = ((), (), s32[]{:S(2)}) async-start(), calls=%async_computation.13 | async-start | bytes 1585152 | tf_op jit(solution)/shard_map/all_gather | solution.py:119
  318.7 170.3 %all-gather.17.cloned.1.call-start = ((), (), s32[]{:S(2)}) async-start(), calls=%async_computation.14 | async-start | bytes 1585152 | tf_op jit(solution)/shard_map/all_gather | solution.py:119
  319.2 252.9 %all-gather.13.cloned.1.call-start = ((), (), s32[]{:S(2)}) async-start(), calls=%async_computation.12 | async-start | bytes 1585152 | tf_op jit(solution)/shard_map/all_gather | solution.py:119
Sparse Core Ops, SparseCore 0:
  10.1 43.5 all-gather.6
  55.7 30.8 all-gather.8
  88.7 31.7 all-gather.10
  273.9 42.5 all-reduce.2
  319.5 86.3 all-gather.14
  409.0 79.8 all-gather.16
  492.1 79.9 all-gather.12
where the time goes:
time: 583 us; the launch traced here: 582 us
  waiting for transfers between devices  410 us (70%)
  starting transfers between devices  90.2 us (15%)
  local copies, waits for them, and re-layouts  29.5 us (5%)
  blocking collectives  15.8 us (3%)
  between operations  15.3 us (3%)
  matrix products  13.1 us (2%)
  other arithmetic  8.61 us (1%)
    all_gather x3, waiting for transfers between devices, shards(): codebook = lax.all_gather(coded, 'rec', axis=0, tiled=True)  247 us
    psum x1, waiting for transfers between devices, shards(): summed, hit_total = lax.psum((partial_value, hit_count), 'grp')  42.7 us
    all_to_all x3, starting transfers between devices, shards(): lax.all_to_all(send_ids.reshape(ranks_total, capacity), 'rec', split_axis...  40 us
    all_to_all x3, waiting for transfers between devices, shards(): lax.all_to_all(send_rows.reshape(ranks_total, capacity, feature_width), '...  38.6 us
    all_gather x3, waiting for transfers between devices, linear(): lax.all_gather(weight, 'grp', axis=1, tiled=True)  35.4 us
    all_to_all x3, waiting for transfers between devices, shards(): lax.all_to_all(send_live.reshape(ranks_total, capacity), 'rec', split_axi...  32.1 us
    all_to_all x3, starting transfers between devices, shards(): lax.all_to_all(send_live.reshape(ranks_total, capacity), 'rec', split_axi...  27.2 us
    all_to_all x3, starting transfers between devices, shards(): lax.all_to_all(send_rows.reshape(ranks_total, capacity, feature_width), '...  19.9 us
  transfers between devices with their start and end apart: 17, of which 13 were waited for; matrix products, arithmetic and copies ran while one was open for 7% of the time, Pallas kernels for 0%

commit v1 on v0

--- a/solution.py
+++ b/solution.py
@@ -116,7 +116,9 @@
         partial_value = jnp.dot(member.T, got_rows, preferred_element_type=jnp.float32)
         hit_count = jnp.sum(member.astype(jnp.float32), axis=0)
         coded = centroid.astype(jnp.bfloat16)
-        codebook = lax.all_gather(coded, "rec", axis=0, tiled=True)
+        codebook = jnp.concatenate(
+            lax.all_to_all(jnp.stack([coded] * lax.axis_size("rec")), "rec", 0, 0), axis=0
+        )
         picked = jnp.take(codebook, chosen, axis=0).astype(jnp.float32)
         gap_value = frames_wide - picked
         results.append(jnp.sum(gap_value * gap_value, axis=1) / feature_width)

time: 583 us -> 493 us (0.85); the launches traced: 582 us -> 484 us
  waiting for transfers between devices: 410 us -> 199 us
  blocking collectives: 15.8 us -> 122 us
  starting transfers between devices: 90.2 us -> 98.6 us
    all_gather x3 -> x0, waiting for transfers between devices: 247 us -> none  [shards(): codebook = lax.all_gather(coded, 'rec', axis=0, tiled=True)]
    all_to_all x0 -> x2, blocking collectives: none -> 106 us  [shards(): lax.all_to_all(jnp.stack([coded] * lax.axis_size('rec')), 'rec', 0, 0)]
    all_to_all x0 -> x1, waiting for transfers between devices: none -> 37.6 us  [shards(): lax.all_to_all(jnp.stack([coded] * lax.axis_size('rec')), 'rec', 0, 0)]
    all_to_all x0 -> x1, starting transfers between devices: none -> 7.71 us  [shards(): lax.all_to_all(jnp.stack([coded] * lax.axis_size('rec')), 'rec', 0, 0)]
  transfers between devices with their start and end apart: 17 -> 15, of which waited for: 13 -> 11; matrix products, arithmetic and copies ran while one was open for 7% -> 8% of each run, Pallas kernels for 0% -> 0%
where the time goes in v1:
time: 493 us; the launch traced here: 484 us
  waiting for transfers between devices  199 us (40%)
  blocking collectives  122 us (25%)
  starting transfers between devices  98.6 us (20%)
  local copies, waits for them, and re-layouts  27.6 us (6%)
  between operations  15.2 us (3%)
  matrix products  13.1 us (3%)
  other arithmetic  8.61 us (2%)
    all_to_all x2, blocking collectives, shards(): lax.all_to_all(jnp.stack([coded] * lax.axis_size('rec')), 'rec', 0, 0)  106 us
    psum x1, waiting for transfers between devices, shards(): summed, hit_total = lax.psum((partial_value, hit_count), 'grp')  42.7 us
    all_to_all x3, starting transfers between devices, shards(): lax.all_to_all(send_ids.reshape(ranks_total, capacity), 'rec', split_axis...  40.6 us
    all_to_all x3, waiting for transfers between devices, shards(): lax.all_to_all(send_rows.reshape(ranks_total, capacity, feature_width), '...  38.5 us
    all_to_all x1, waiting for transfers between devices, shards(): lax.all_to_all(jnp.stack([coded] * lax.axis_size('rec')), 'rec', 0, 0)  37.6 us
    all_gather x3, waiting for transfers between devices, linear(): lax.all_gather(weight, 'grp', axis=1, tiled=True)  34.8 us
    all_to_all x3, waiting for transfers between devices, shards(): lax.all_to_all(send_live.reshape(ranks_total, capacity), 'rec', split_axi...  32.1 us
    all_to_all x3, starting transfers between devices, shards(): lax.all_to_all(send_live.reshape(ranks_total, capacity), 'rec', split_axi...  27.2 us
  transfers between devices with their start and end apart: 15, of which 11 were waited for; matrix products, arithmetic and copies ran while one was open for 8% of the time, Pallas kernels for 0%

profile of v1, /device:TPU:1, one launch (start us, length us, event | category | flops | bytes accessed | tf_op | source)
XLA Modules:
  0.0 483.6 jit_solution(5708602719484677502)
XLA Ops:
  12.4 18.4 %all-to-all-start.5 = ((s32[128,1,2]{2,1,0:T(1,128)}), s32[128,1,2]{2,1,0:T(1,128)S(1)}, u32[]{:S(2)}, u32[]{:S(2)}) async-start(s32[128,1,2]{2,1,0:T(1,128)} %bitcast.18), calls=%async_computation.5 | async-start | bytes 131072 | tf_op jit(solution)/shard_map/all_to_all | solution.py:95
  34.4 15.8 %all_gather.15 = bf16[512,768]{0,1:T(8,128)(2,1)S(1)} all-gather(bf16[512,192]{0,1:T(8,128)(2,1)} %param.20), channel_id=1, replica_groups=mesh['rec'=128,'grp'=4] {'grp'}, dimensions={1}, use_global_device_ids=true | all-gather | bytes 983040 | tf_op jit(solution)/shard_map/all_gather | solution.py:19
  66.3 20.3 %all-gather.6.cloned.1.call-done = bf16[1024,512]{1,0:T(8,128)(2,1)} async-done(((bf16[1024,128]{1,0:T(8,128)(2,1)}), bf16[1024,512]{1,0:T(8,128)(2,1)}) %all-gather.6.cloned.1.call-update) | async-done | bytes 1048592 | tf_op jit(solution)/shard_map/all_gather | solution.py:19
  89.4 16.5 %all-to-all-start.9 = ((s32[128,1,2]{2,1,0:T(1,128)}), s32[128,1,2]{2,1,0:T(1,128)S(1)}, u32[]{:S(2)}, u32[]{:S(2)}) async-start(s32[128,1,2]{2,1,0:T(1,128)} %bitcast.26), calls=%async_computation.9 | async-start | bytes 131072 | tf_op jit(solution)/shard_map/all_to_all | solution.py:95
  105.9 14.5 %all-gather.8.cloned.1.call-done = bf16[1024,512]{1,0:T(8,128)(2,1)} async-done(((bf16[1024,128]{1,0:T(8,128)(2,1)}), bf16[1024,512]{1,0:T(8,128)(2,1)}) %all-gather.8.cloned.1.call-update) | async-done | bytes 1048592 | tf_op jit(solution)/shard_map/all_gather | solution.py:19
  122.6 15.9 %all-to-all-start.6 = ((s32[128,1,2]{2,1,0:T(1,128)}), s32[128,1,2]{2,1,0:T(1,128)S(1)}, u32[]{:S(2)}, u32[]{:S(2)}) async-start(s32[128,1,2]{2,1,0:T(1,128)} %bitcast.19), calls=%async_computation.6 | async-start | bytes 131072 | tf_op jit(solution)/shard_map/all_to_all | solution.py:102
  138.5 11.5 %all-to-all-done.6 = s32[128,1,2]{2,1,0:T(1,128)S(1)} async-done(((s32[128,1,2]{2,1,0:T(1,128)}), s32[128,1,2]{2,1,0:T(1,128)S(1)}, u32[]{:S(2)}, u32[]{:S(2)}) %all-to-all-start.6) | async-done | bytes 1056 | tf_op jit(solution)/shard_map/all_to_all | solution.py:102
  150.1 5.6 %all-to-all-start.10 = ((s32[128,1,2]{2,1,0:T(1,128)}), s32[128,1,2]{2,1,0:T(1,128)S(1)}, u32[]{:S(2)}, u32[]{:S(2)}) async-start(s32[128,1,2]{2,1,0:T(1,128)} %bitcast.27), calls=%async_computation.10 | async-start | bytes 131072 | tf_op jit(solution)/shard_map/all_to_all | solution.py:102
  155.9 11.5 %all-to-all-done.10 = s32[128,1,2]{2,1,0:T(1,128)S(1)} async-done(((s32[128,1,2]{2,1,0:T(1,128)}), s32[128,1,2]{2,1,0:T(1,128)S(1)}, u32[]{:S(2)}, u32[]{:S(2)}) %all-to-all-start.10) | async-done | bytes 1056 | tf_op jit(solution)/shard_map/all_to_all | solution.py:102
  167.4 5.7 %all-to-all-start.1 = ((s32[128,1,2]{2,1,0:T(1,128)}), s32[128,1,2]{2,1,0:T(1,128)S(1)}, u32[]{:S(2)}, u32[]{:S(2)}) async-start(s32[128,1,2]{2,1,0:T(1,128)} %bitcast.9), calls=%async_computation.1 | async-start | bytes 131072 | tf_op jit(solution)/shard_map/all_to_all | solution.py:95
  173.1 11.7 %all-to-all-done.1 = s32[128,1,2]{2,1,0:T(1,128)S(1)} async-done(((s32[128,1,2]{2,1,0:T(1,128)}), s32[128,1,2]{2,1,0:T(1,128)S(1)}, u32[]{:S(2)}, u32[]{:S(2)}) %all-to-all-start.1) | async-done | bytes 1056 | tf_op jit(solution)/shard_map/all_to_all | solution.py:95
  184.8 5.7 %all-to-all-start.2 = ((s32[128,1,2]{2,1,0:T(1,128)}), s32[128,1,2]{2,1,0:T(1,128)S(1)}, u32[]{:S(2)}, u32[]{:S(2)}) async-start(s32[128,1,2]{2,1,0:T(1,128)} %bitcast.11), calls=%async_computation.2 | async-start | bytes 131072 | tf_op jit(solution)/shard_map/all_to_all | solution.py:102
  193.0 9.1 %all-to-all-done.2 = s32[128,1,2]{2,1,0:T(1,128)S(1)} async-done(((s32[128,1,2]{2,1,0:T(1,128)}), s32[128,1,2]{2,1,0:T(1,128)S(1)}, u32[]{:S(2)}, u32[]{:S(2)}) %all-to-all-start.2) | async-done | bytes 1056 | tf_op jit(solution)/shard_map/all_to_all | solution.py:102
  202.1 6.0 %all-to-all-start.7 = ((bf16[128,2,768]{2,1,0:T(2,128)(2,1)}), bf16[128,2,768]{2,1,0:T(2,128)(2,1)S(1)}, u32[]{:S(2)}, u32[]{:S(2)}) async-start(bf16[128,2,768]{2,1,0:T(2,128)(2,1)} %reshape.467), calls=%async_computation.7 | async-start | bytes 786432 | tf_op jit(solution)/shard_map/all_to_all | solution.py:88
  210.3 14.7 %all-to-all-done.7 = bf16[128,2,768]{2,1,0:T(2,128)(2,1)S(1)} async-done(((bf16[128,2,768]{2,1,0:T(2,128)(2,1)}), bf16[128,2,768]{2,1,0:T(2,128)(2,1)S(1)}, u32[]{:S(2)}, u32[]{:S(2)}) %all-to-all-start.7) | async-done | bytes 393248 | tf_op jit(solution)/shard_map/all_to_all | solution.py:88
  224.9 7.1 %all-to-all-start.11 = ((bf16[128,2,768]{2,1,0:T(2,128)(2,1)}), bf16[128,2,768]{2,1,0:T(2,128)(2,1)S(1)}, u32[]{:S(2)}, u32[]{:S(2)}) async-start(bf16[128,2,768]{2,1,0:T(2,128)(2,1)} %reshape.470), calls=%async_computation.11 | async-start | bytes 786432 | tf_op jit(solution)/shard_map/all_to_all | solution.py:88
  238.3 10.7 %all-to-all-done.11 = bf16[128,2,768]{2,1,0:T(2,128)(2,1)S(1)} async-done(((bf16[128,2,768]{2,1,0:T(2,128)(2,1)}), bf16[128,2,768]{2,1,0:T(2,128)(2,1)S(1)}, u32[]{:S(2)}, u32[]{:S(2)}) %all-to-all-start.11) | async-done | bytes 393248 | tf_op jit(solution)/shard_map/all_to_all | solution.py:88
  248.9 7.1 %all-to-all-start.3 = ((bf16[128,2,768]{2,1,0:T(2,128)(2,1)}), bf16[128,2,768]{2,1,0:T(2,128)(2,1)S(1)}, u32[]{:S(2)}, u32[]{:S(2)}) async-start(bf16[128,2,768]{2,1,0:T(2,128)(2,1)} %reshape.464), calls=%async_computation.3 | async-start | bytes 786432 | tf_op jit(solution)/shard_map/all_to_all | solution.py:88
  259.7 13.2 %all-to-all-done.3 = bf16[128,2,768]{2,1,0:T(2,128)(2,1)S(1)} async-done(((bf16[128,2,768]{2,1,0:T(2,128)(2,1)}), bf16[128,2,768]{2,1,0:T(2,128)(2,1)S(1)}, u32[]{:S(2)}, u32[]{:S(2)}) %all-to-all-start.3) | async-done | bytes 393248 | tf_op jit(solution)/shard_map/all_to_all | solution.py:88
  273.9 42.7 %all-reduce.3.cloned.1.call-done = (f32[8]{0:T(128)}, f32[8,768]{1,0:T(8,128)}, f32[8,768]{1,0:T(8,128)}, f32[8]{0:T(128)}, f32[8,768]{1,0:T(8,128)}, /*index=5*/f32[8]{0:T(128)}) async-done(((f32[8]{0:T(128)}, f32[8,768]{1,0:T(8,128)}, f32[8,768]{1,0:T(8,128)}, f32[8]{0:T(128)}, f32[8,768]{1,0:T(8,128)}, /*index=5*/f32[8]{0:T(128)}), (f32[8]{0:T(128)}, f32[8,768]{1,0:T(8,128)}, f32[8,768]{1,0:T(8,128)}, ...) | async-done | bytes 73840 | tf_op jit(solution)/shard_map/psum | solution.py:125
  318.9 57.2 %all_to_all.84 = bf16[128,8,768]{2,1,0:T(8,128)(2,1)S(1)} all-to-all(bf16[128,8,768]{2,1,0:T(8,128)(2,1)S(1)} %stack.9), channel_id=1, replica_groups=mesh['rec'=128,'grp'=4] {'rec'}, dimensions={0} | all-to-all | bytes 3145728 | tf_op jit(solution)/shard_map/all_to_all | solution.py:120
  376.2 48.6 %all_to_all.85 = bf16[128,8,768]{2,1,0:T(8,128)(2,1)} all-to-all(bf16[128,8,768]{2,1,0:T(8,128)(2,1)S(1)} %stack.10), channel_id=1, replica_groups=mesh['rec'=128,'grp'=4] {'rec'}, dimensions={0} | all-to-all | bytes 3145728 | tf_op jit(solution)/shard_map/all_to_all | solution.py:120
  426.1 7.7 %all-to-all-start = ((bf16[128,8,768]{2,1,0:T(8,128)(2,1)}), bf16[128,8,768]{2,1,0:T(8,128)(2,1)S(1)}, u32[]{:S(2)}, u32[]{:S(2)}) async-start(bf16[128,8,768]{2,1,0:T(8,128)(2,1)} %stack.8), calls=%async_computation | async-start | bytes 3145728 | tf_op jit(solution)/shard_map/all_to_all | solution.py:120
  437.4 37.6 %all-to-all-done = bf16[128,8,768]{2,1,0:T(8,128)(2,1)S(1)} async-done(((bf16[128,8,768]{2,1,0:T(8,128)(2,1)}), bf16[128,8,768]{2,1,0:T(8,128)(2,1)S(1)}, u32[]{:S(2)}, u32[]{:S(2)}) %all-to-all-start) | async-done | bytes 1572896 | tf_op jit(solution)/shard_map/all_to_all | solution.py:120
  (105 shorter events, 53.7 us)
Async XLA Ops:
  7.2 43.7 %copy-start = (bf16[1,1024,512]{2,1,0:T(8,128)(2,1)S(1)}, bf16[1,1024,512]{2,1,0:T(8,128)(2,1)}, u32[]{:S(2)}) copy-start(bf16[1,1024,512]{2,1,0:T(8,128)(2,1)} %param.14) | copy-start | bytes 3145732
  7.2 54.0 %all-gather.4.cloned.1.call-start = ((), (), s32[]{:S(2)}) async-start(), calls=%async_computation.12 | async-start | bytes 1966080 | tf_op jit(solution)/shard_map/all_gather | solution.py:19
  7.9 78.7 %all-gather.6.cloned.1.call-start = ((), (), s32[]{:S(2)}) async-start(), calls=%async_computation.13 | async-start | bytes 1310720 | tf_op jit(solution)/shard_map/all_gather | solution.py:19
  12.4 77.0 %all-to-all-start.5 = ((s32[128,1,2]{2,1,0:T(1,128)}), s32[128,1,2]{2,1,0:T(1,128)S(1)}, u32[]{:S(2)}, u32[]{:S(2)}) async-start(s32[128,1,2]{2,1,0:T(1,128)} %bitcast.18), calls=%async_computation.5 | async-start | bytes 131072 | tf_op jit(solution)/shard_map/all_to_all | solution.py:95
  30.8 89.6 %all-gather.8.cloned.1.call-start = ((), (), s32[]{:S(2)}) async-start(), calls=%async_computation.14 | async-start | bytes 1310720 | tf_op jit(solution)/shard_map/all_gather | solution.py:19
  31.6 29.6 %collective-permute-start = (bf16[1,512]{1,0:T(2,128)(2,1)S(1)}, bf16[1,512]{1,0:T(2,128)(2,1)S(1)}, u32[]{:S(2)}, u32[]{:S(2)}) collective-permute-start(bf16[1,512]{1,0:T(2,128)(2,1)S(1)} %slice_bitcast_fusion), channel_id=1, source_target_pairs={{4,0},{8,4},{12,8},{16,12},{20,16},{24,20},{28,24},{32,28},{36,32}... | collective-permute-start | bytes 3080 | tf_op jit(solution)/shard_map/ppermute | solution.py:13
  89.4 33.2 %all-to-all-start.9 = ((s32[128,1,2]{2,1,0:T(1,128)}), s32[128,1,2]{2,1,0:T(1,128)S(1)}, u32[]{:S(2)}, u32[]{:S(2)}) async-start(s32[128,1,2]{2,1,0:T(1,128)} %bitcast.26), calls=%async_computation.9 | async-start | bytes 131072 | tf_op jit(solution)/shard_map/all_to_all | solution.py:95
  105.9 84.6 %copy-start.6 = (f32[768]{0:T(1024)S(1)}, f32[768]{0:T(1024)}, u32[]{:S(2)}) copy-start(f32[768]{0:T(1024)} %param.21) | copy-start | bytes 9220
  105.9 84.6 %copy-start.7 = (f32[512]{0:T(512)S(1)}, f32[512]{0:T(512)}, u32[]{:S(2)}) copy-start(f32[512]{0:T(512)} %param.19) | copy-start | bytes 6148
  105.9 84.6 %copy-start.8 = (f32[512]{0:T(512)S(1)}, f32[512]{0:T(512)}, u32[]{:S(2)}) copy-start(f32[512]{0:T(512)} %param.18) | copy-start | bytes 6148
  122.6 27.4 %all-to-all-start.6 = ((s32[128,1,2]{2,1,0:T(1,128)}), s32[128,1,2]{2,1,0:T(1,128)S(1)}, u32[]{:S(2)}, u32[]{:S(2)}) async-start(s32[128,1,2]{2,1,0:T(1,128)} %bitcast.19), calls=%async_computation.6 | async-start | bytes 131072 | tf_op jit(solution)/shard_map/all_to_all | solution.py:102
  150.1 17.3 %all-to-all-start.10 = ((s32[128,1,2]{2,1,0:T(1,128)}), s32[128,1,2]{2,1,0:T(1,128)S(1)}, u32[]{:S(2)}, u32[]{:S(2)}) async-start(s32[128,1,2]{2,1,0:T(1,128)} %bitcast.27), calls=%async_computation.10 | async-start | bytes 131072 | tf_op jit(solution)/shard_map/all_to_all | solution.py:102
  167.4 17.4 %all-to-all-start.1 = ((s32[128,1,2]{2,1,0:T(1,128)}), s32[128,1,2]{2,1,0:T(1,128)S(1)}, u32[]{:S(2)}, u32[]{:S(2)}) async-start(s32[128,1,2]{2,1,0:T(1,128)} %bitcast.9), calls=%async_computation.1 | async-start | bytes 131072 | tf_op jit(solution)/shard_map/all_to_all | solution.py:95
  184.8 17.3 %all-to-all-start.2 = ((s32[128,1,2]{2,1,0:T(1,128)}), s32[128,1,2]{2,1,0:T(1,128)S(1)}, u32[]{:S(2)}, u32[]{:S(2)}) async-start(s32[128,1,2]{2,1,0:T(1,128)} %bitcast.11), calls=%async_computation.2 | async-start | bytes 131072 | tf_op jit(solution)/shard_map/all_to_all | solution.py:102
  190.9 45.2 %copy-start.1 = (bf16[128,768]{1,0:T(8,128)(2,1)}, bf16[128,768]{1,0:T(8,128)(2,1)S(1)}, u32[]{:S(2)}) copy-start(bf16[128,768]{1,0:T(8,128)(2,1)S(1)} %fusion.6) | copy-start | bytes 589828
  202.1 22.8 %all-to-all-start.7 = ((bf16[128,2,768]{2,1,0:T(2,128)(2,1)}), bf16[128,2,768]{2,1,0:T(2,128)(2,1)S(1)}, u32[]{:S(2)}, u32[]{:S(2)}) async-start(bf16[128,2,768]{2,1,0:T(2,128)(2,1)} %reshape.467), calls=%async_computation.7 | async-start | bytes 786432 | tf_op jit(solution)/shard_map/all_to_all | solution.py:88
  224.9 24.0 %all-to-all-start.11 = ((bf16[128,2,768]{2,1,0:T(2,128)(2,1)}), bf16[128,2,768]{2,1,0:T(2,128)(2,1)S(1)}, u32[]{:S(2)}, u32[]{:S(2)}) async-start(bf16[128,2,768]{2,1,0:T(2,128)(2,1)} %reshape.470), calls=%async_computation.11 | async-start | bytes 786432 | tf_op jit(solution)/shard_map/all_to_all | solution.py:88
  248.9 24.0 %all-to-all-start.3 = ((bf16[128,2,768]{2,1,0:T(2,128)(2,1)}), bf16[128,2,768]{2,1,0:T(2,128)(2,1)S(1)}, u32[]{:S(2)}, u32[]{:S(2)}) async-start(bf16[128,2,768]{2,1,0:T(2,128)(2,1)} %reshape.464), calls=%async_computation.3 | async-start | bytes 786432 | tf_op jit(solution)/shard_map/all_to_all | solution.py:88
  256.1 60.6 %all-reduce.3.cloned.1.call-start = ((), (), s32[]{:S(2)}) async-start(), calls=%async_computation.15 | async-start | bytes 150528 | tf_op jit(solution)/shard_map/psum | solution.py:125
  258.0 58.7 %copy-start.5 = (f32[8]{0:T(128)S(1)}, f32[8]{0:T(128)}, u32[]{:S(2)}) copy-start(f32[8]{0:T(128)} %param.25) | copy-start | bytes 100
  258.0 59.3 %copy-start.3 = (f32[8,768]{1,0:T(8,128)S(1)}, f32[8,768]{1,0:T(8,128)}, u32[]{:S(2)}) copy-start(f32[8,768]{1,0:T(8,128)} %param.24) | copy-start | bytes 73732
  426.1 7.7 %copy-start.4 = (s32[3,1,128]{2,1,0:T(1,128)S(1)}, s32[3,1,128]{2,1,0:T(1,128)}, u32[]{:S(2)}) copy-start(s32[3,1,128]{2,1,0:T(1,128)} %param.23) | copy-start | bytes 4612
  426.1 48.8 %all-to-all-start = ((bf16[128,8,768]{2,1,0:T(8,128)(2,1)}), bf16[128,8,768]{2,1,0:T(8,128)(2,1)S(1)}, u32[]{:S(2)}, u32[]{:S(2)}) async-start(bf16[128,8,768]{2,1,0:T(8,128)(2,1)} %stack.8), calls=%async_computation | async-start | bytes 3145728 | tf_op jit(solution)/shard_map/all_to_all | solution.py:120
  434.7 41.1 %copy-start.2 = (bf16[128,768]{1,0:T(8,128)(2,1)S(1)}, bf16[128,768]{1,0:T(8,128)(2,1)}, u32[]{:S(2)}) copy-start(bf16[128,768]{1,0:T(8,128)(2,1)} %copy-done.1) | copy-start | bytes 589828
Sparse Core Ops, SparseCore 0:
  10.1 43.5 all-gather.3
  55.7 30.8 all-gather.5
  88.7 31.6 all-gather.7
  274.1 42.5 all-reduce.2
